TPU v7x, 32 devices: a whole 2x2x4 slice. The times are simulated.
32 devices in a mesh: batch: 4 (over y, x), seq: 4 (over z), head: 2 (over core).
Axes of the slice: x: 2, y: 2, z: 4, core: 2. Of those that a mesh axis runs over, the one named last changes fastest.
Arguments:
- hidden: bfloat16 [4, 2048, 1024], P('batch', 'seq', 'head'), may hold values from -6 to 6
- norm_gain: bfloat16 [1024], P('head'), may hold values from 0.099609375 to 1.8984375
- gate_weight: bfloat16 [1024, 2048], P(None, 'head'), may hold values from -0.1875 to 0.1875
- inner_weight: bfloat16 [1024, 2048], P(None, 'head'), may hold values from -0.1875 to 0.1875
- step_weight: bfloat16 [1024, 32], P(None, 'head'), may hold values from -0.375 to 0.375
- maps_weight: bfloat16 [1024, 256], replicated, may hold values from -0.1875 to 0.1875
- inner_kernel: float32 [4, 2048], P(None, 'head'), may hold values from -3 to 3
- inner_bias: float32 [2048], P('head'), may hold values from -1 to 1
- maps_kernel: float32 [4, 256], replicated, may hold values from -3 to 3
- maps_bias: float32 [256], replicated, may hold values from -1 to 1
- step_bias: float32 [32], P('head'), may hold values from -7 to -5
- decay_log: float32 [32], P('head'), may hold values from -5.3 to 1
- skip_gain: float32 [32], P('head'), may hold values from 1 to 4
- gate_gain: float32 [2048], P('head'), may hold values from 0.1 to 1.9
- output_weight: bfloat16 [2048, 1024], P('head'), may hold values from -0.125 to 0.125
- cotangent: bfloat16 [4, 2048, 1024], P('batch', 'seq', 'head'), may hold values from -6 to 6
Outputs:
- output: float32 [4, 2048, 1024], P('batch', 'seq', 'head')
- grad_hidden: float32 [4, 2048, 1024], P('batch', 'seq', 'head')
- grad_norm_gain: float32 [1024], P('head')
- grad_gate_weight: float32 [1024, 2048], P(None, 'head')
- grad_inner_weight: float32 [1024, 2048], P(None, 'head')
- grad_step_weight: float32 [1024, 32], P(None, 'head')
- grad_maps_weight: float32 [1024, 256], replicated
- grad_inner_kernel: float32 [4, 2048], P(None, 'head')
- grad_inner_bias: float32 [2048], P('head')
- grad_maps_kernel: float32 [4, 256], replicated
- grad_maps_bias: float32 [256], replicated
- grad_step_bias: float32 [32], P('head')
- grad_decay_log: float32 [32], P('head')
- grad_skip_gain: float32 [32], P('head')
- grad_gate_gain: float32 [2048], P('head')
- grad_output_weight: float32 [2048, 1024], P('head')
All inputs are finite; a program needn't handle non-finite values.
Results may differ from a plain program's by a relative error of at most 0.0089.
Values may be sent and summed in bfloat16 or wider, within the bound.
A program may use at most 192 MiB of HBM per device.

v0:
```python
import jax
import jax.numpy as jnp
from jax import lax
from jax.sharding import PartitionSpec as P

D = 1024
HEADDIM = 64
STATE = 128
CONV = 4
GROUP = 256
DI = 2048
HIGH = lax.Precision.HIGHEST
EPSILON = 1e-05


def shifted(array, axis, by):
    count = lax.axis_size(axis)
    pairs = [(i, i + by) for i in range(count) if 0 <= i + by < count]
    return lax.ppermute(array, axis, pairs)


def entering(array, axis, combine, identity, reverse):
    count, index = (lax.axis_size(axis), lax.axis_index(axis))
    everything = jax.tree.map(lambda part: lax.all_gather(part, axis), array)
    start = jax.tree.map(
        lambda part, zero: jnp.broadcast_to(jnp.asarray(zero, part.dtype), part.shape),
        array,
        identity,
    )

    def step(k, before):
        at = count - 1 - k if reverse else k
        reached = at > index if reverse else at < index
        new = combine(before, jax.tree.map(lambda part: part[at], everything))
        return jax.tree.map(lambda a, b: jnp.where(reached, a, b), new, before)

    return lax.fori_loop(0, count, step, start)


def silu_slope(values):
    sigmoid = jax.nn.sigmoid(values)
    return sigmoid * (1.0 + values * (1.0 - sigmoid))


def ssd_blocks(inner_act, write_map, read_map, step_size, decay_rates, initial):
    length, heads, headdim = inner_act.shape
    blocks_count = length // GROUP
    inner_blocks = inner_act.reshape(blocks_count, GROUP, heads, headdim)
    write_blocks = write_map.reshape(blocks_count, GROUP, write_map.shape[-1])
    read_blocks = read_map.reshape(blocks_count, GROUP, read_map.shape[-1])
    step_blocks = step_size.reshape(blocks_count, GROUP, heads)
    causal = (jnp.arange(GROUP)[:, None] >= jnp.arange(GROUP)[None, :])[:, :, None]

    def advance(state_in, pieces):
        inner_part, write_part, read_part, step_part = pieces
        cumlog = jnp.cumsum(step_part * decay_rates[None, :], axis=0)
        spread = jnp.where(causal, cumlog[:, None, :] - cumlog[None, :, :], 0.0)
        decays = jnp.where(causal, jnp.exp(spread), 0.0)
        scores = jnp.dot(read_part, write_part.T, precision=HIGH)
        weighted = inner_part * step_part[:, :, None]
        within = jnp.einsum("tsh,shp->thp", decays * scores[:, :, None], weighted, precision=HIGH)
        carried = jnp.einsum("tn,hpn->thp", read_part, state_in, precision=HIGH)
        result = within + jnp.exp(cumlog)[:, :, None] * carried
        remain = jnp.exp(cumlog[-1][None, :] - cumlog)
        fresh = jnp.einsum("shp,sn->hpn", weighted * remain[:, :, None], write_part, precision=HIGH)
        state_out = jnp.exp(cumlog[-1])[:, None, None] * state_in + fresh
        return (state_out, result)

    final, outputs = lax.scan(
        advance, initial, (inner_blocks, write_blocks, read_blocks, step_blocks)
    )
    return (outputs.reshape(length, heads, headdim), final)


def batched_scan(inner_heads, write_map, read_map, step_size, decay_rates, state_in):
    return jax.vmap(ssd_blocks, in_axes=(0, 0, 0, 0, None, 0))(
        inner_heads, write_map, read_map, step_size, decay_rates, state_in
    )


def chain_pair(earlier, later):
    return (earlier[0] * later[0], earlier[1] * later[0][:, :, None, None] + later[1])


def conv_apply(padded, kernel, bias_row, length):
    summed = bias_row
    for offset in range(kernel.shape[0]):
        summed = summed + kernel[offset] * padded[..., offset : offset + length, :]
    return summed


def conv_grads(padded, extended, grad_out, kernel, length):
    leading = tuple(range(grad_out.ndim - 1))
    grad_kernel = jnp.stack(
        [
            jnp.sum(grad_out * padded[..., offset : offset + length, :], axis=leading)
            for offset in range(kernel.shape[0])
        ]
    )
    grad_bias = jnp.sum(grad_out, axis=leading)
    width_less = kernel.shape[0] - 1
    grad_input = jnp.zeros_like(grad_out)
    for offset in range(kernel.shape[0]):
        begin_at = width_less - offset
        grad_input = grad_input + kernel[offset] * extended[..., begin_at : begin_at + length, :]
    return (grad_input, grad_kernel, grad_bias)


def on_device(
    hidden,
    norm_gain,
    gate_weight,
    inner_weight,
    step_weight,
    maps_weight,
    inner_kernel,
    inner_bias,
    maps_kernel,
    maps_bias,
    step_bias,
    decay_log,
    skip_gain,
    gate_gain,
    output_weight,
    cotangent,
):
    seq_count, tok_count, local_width = hidden.shape
    rows_count = seq_count * tok_count
    local_inner = gate_weight.shape[1]
    heads_local = step_weight.shape[1]
    whole_hidden, whole_cotangent, whole_gain = (
        lax.all_gather(hidden, "head", axis=2, tiled=True),
        lax.all_gather(cotangent, "head", axis=2, tiled=True),
        lax.all_gather(norm_gain, "head", axis=0, tiled=True),
    )
    residual = whole_hidden.reshape(rows_count, D).astype(jnp.float32)
    inverse = lax.rsqrt(jnp.mean(residual * residual, axis=-1, keepdims=True) + EPSILON)
    normal = residual * inverse
    normed = (normal * whole_gain.astype(jnp.float32)).astype(jnp.bfloat16)
    gate_pre = jnp.dot(normed, gate_weight, preferred_element_type=jnp.float32)
    inner_pre = jnp.dot(normed, inner_weight, preferred_element_type=jnp.float32)
    maps_pre = jnp.dot(normed, maps_weight, preferred_element_type=jnp.float32)
    step_pre = jnp.dot(normed, step_weight, preferred_element_type=jnp.float32).reshape(
        seq_count, tok_count, heads_local
    )
    inner_seq = inner_pre.reshape(seq_count, tok_count, local_inner)
    maps_seq = maps_pre.reshape(seq_count, tok_count, 2 * STATE)
    edge_inner, edge_maps = shifted(
        (inner_seq[:, tok_count - (CONV - 1) :, :], maps_seq[:, tok_count - (CONV - 1) :, :]),
        "seq",
        1,
    )
    inner_pad = jnp.concatenate([edge_inner, inner_seq], axis=1)
    maps_pad = jnp.concatenate([edge_maps, maps_seq], axis=1)
    inner_conv = conv_apply(inner_pad, inner_kernel, inner_bias, tok_count)
    maps_conv = conv_apply(maps_pad, maps_kernel, maps_bias, tok_count)
    inner_act = jax.nn.silu(inner_conv)
    maps_act = jax.nn.silu(maps_conv)
    write_map = maps_act[..., :STATE]
    read_map = maps_act[..., STATE:]
    step_size = jax.nn.softplus(step_pre + step_bias)
    decay_rates = -jnp.exp(decay_log)
    inner_heads = inner_act.reshape(seq_count, tok_count, heads_local, HEADDIM)
    zero_state = jnp.zeros((seq_count, heads_local, HEADDIM, STATE), jnp.float32)
    local_mix, local_state = batched_scan(
        inner_heads, write_map, read_map, step_size, decay_rates, zero_state
    )
    cumlog = jnp.cumsum(step_size * decay_rates, axis=1)
    total_decay = jnp.exp(cumlog[:, -1, :])
    identity = (jnp.ones_like(total_decay), jnp.zeros_like(local_state))
    prefix_decay, state_in = entering(
        (total_decay, local_state), "seq", chain_pair, identity, False
    )
    carried = jnp.einsum("stn,shpn->sthp", read_map, state_in, precision=HIGH)
    mixed_out = (
        local_mix
        + jnp.exp(cumlog)[..., None] * carried
        + skip_gain[None, None, :, None] * inner_heads
    )
    mixed_flat = mixed_out.reshape(rows_count, local_inner)
    gate_act = jax.nn.silu(gate_pre)
    gated_val = mixed_flat * gate_act
    square_total = lax.psum(jnp.sum(gated_val * gated_val, axis=-1), "head")
    scale_back = lax.rsqrt(square_total[:, None] / DI + EPSILON)
    gated_norm = (gated_val * scale_back * gate_gain).astype(jnp.bfloat16)
    branch_part = jnp.dot(gated_norm, output_weight, preferred_element_type=jnp.float32)
    branch = lax.psum_scatter(branch_part, "head", scatter_dimension=1, tiled=True)
    output = (hidden.reshape(rows_count, local_width).astype(jnp.float32) + branch).reshape(
        seq_count, tok_count, local_width
    )
    cot_rows = whole_cotangent.reshape(rows_count, D)
    grad_output_weight = jnp.dot(gated_norm.T, cot_rows, preferred_element_type=jnp.float32)
    grad_norm_out = jnp.dot(cot_rows, output_weight.T, preferred_element_type=jnp.float32)
    grad_gate_gain = jnp.sum(grad_norm_out * gated_val * scale_back, axis=0)
    grad_scaled = grad_norm_out * gate_gain
    dot_total = lax.psum(jnp.sum(grad_scaled * gated_val, axis=-1), "head")
    grad_gated = scale_back * (
        grad_scaled - gated_val * scale_back * scale_back * (dot_total[:, None] / DI)
    )
    grad_mixed = (grad_gated * gate_act).reshape(seq_count, tok_count, heads_local, HEADDIM)
    grad_gate_pre = grad_gated * mixed_flat * silu_slope(gate_pre)
    grad_skip_gain = jnp.sum(grad_mixed * inner_heads, axis=(0, 1, 3))
    from_here = jnp.einsum(
        "sthp,stn->shpn", grad_mixed * jnp.exp(cumlog)[..., None], read_map, precision=HIGH
    )
    suffix_decay, state_grad = entering((total_decay, from_here), "seq", chain_pair, identity, True)
    recomputed, scan_back = jax.vjp(
        batched_scan, inner_heads, write_map, read_map, step_size, decay_rates, state_in
    )
    grad_inner_heads, grad_write, grad_read, grad_step, grad_rates, grad_start = scan_back(
        (grad_mixed, state_grad)
    )
    grad_write, grad_read = lax.psum((grad_write, grad_read), "head")
    grad_maps = jnp.concatenate([grad_write, grad_read], axis=-1)
    grad_inner = (grad_inner_heads + skip_gain[None, None, :, None] * grad_mixed).reshape(
        seq_count, tok_count, local_inner
    )
    grad_inner_conv = grad_inner * silu_slope(inner_conv)
    grad_maps_conv = grad_maps * silu_slope(maps_conv)
    next_inner, next_maps = shifted(
        (grad_inner_conv[:, : CONV - 1, :], grad_maps_conv[:, : CONV - 1, :]), "seq", -1
    )
    inner_ext = jnp.concatenate([grad_inner_conv, next_inner], axis=1)
    maps_ext = jnp.concatenate([grad_maps_conv, next_maps], axis=1)
    grad_inner_pre, grad_inner_kernel, grad_inner_bias = conv_grads(
        inner_pad, inner_ext, grad_inner_conv, inner_kernel, tok_count
    )
    grad_maps_pre, grad_maps_kernel, grad_maps_bias = conv_grads(
        maps_pad, maps_ext, grad_maps_conv, maps_kernel, tok_count
    )
    grad_step_pre = grad_step * jax.nn.sigmoid(step_pre + step_bias)
    grad_step_bias = jnp.sum(grad_step_pre, axis=(0, 1))
    grad_decay_log = grad_rates * decay_rates
    gate_round = grad_gate_pre.astype(jnp.bfloat16)
    inner_round = grad_inner_pre.reshape(rows_count, local_inner).astype(jnp.bfloat16)
    maps_round = grad_maps_pre.reshape(rows_count, 2 * STATE).astype(jnp.bfloat16)
    step_round = grad_step_pre.reshape(rows_count, heads_local).astype(jnp.bfloat16)
    grad_gate_weight = jnp.dot(normed.T, gate_round, preferred_element_type=jnp.float32)
    grad_inner_weight = jnp.dot(normed.T, inner_round, preferred_element_type=jnp.float32)
    grad_maps_weight = jnp.dot(normed.T, maps_round, preferred_element_type=jnp.float32)
    grad_step_weight = jnp.dot(normed.T, step_round, preferred_element_type=jnp.float32)
    partial_normed = jnp.dot(gate_round, gate_weight.T, preferred_element_type=jnp.float32)
    partial_normed = partial_normed + jnp.dot(
        inner_round, inner_weight.T, preferred_element_type=jnp.float32
    )
    partial_normed = partial_normed + jnp.dot(
        step_round, step_weight.T, preferred_element_type=jnp.float32
    )
    input_share = lax.psum_scatter(partial_normed, "head", scatter_dimension=1, tiled=True)
    column_start = lax.axis_index("head") * local_width
    maps_rows = lax.dynamic_slice_in_dim(maps_weight, column_start, local_width, 0)
    input_share = input_share + jnp.dot(maps_round, maps_rows.T, preferred_element_type=jnp.float32)
    normal_local = lax.dynamic_slice_in_dim(normal, column_start, local_width, 1)
    grad_normal = input_share * norm_gain.astype(jnp.float32)
    dot_sum = lax.psum(jnp.sum(grad_normal * normal_local, axis=-1), "head")
    grad_rows = inverse * (grad_normal - normal_local * (dot_sum[:, None] / D)) + cotangent.reshape(
        rows_count, local_width
    ).astype(jnp.float32)
    grad_hidden = grad_rows.reshape(seq_count, tok_count, local_width)
    grad_norm_gain = jnp.sum(input_share * normal_local, axis=0)
    summed = lax.psum(
        (
            grad_norm_gain,
            grad_gate_weight,
            grad_inner_weight,
            grad_step_weight,
            grad_maps_weight,
            grad_inner_kernel,
            grad_inner_bias,
            grad_maps_kernel,
            grad_maps_bias,
            grad_step_bias,
            grad_decay_log,
            grad_skip_gain,
            grad_gate_gain,
            grad_output_weight,
        ),
        ("batch", "seq"),
    )
    return (
        output,
        grad_hidden,
        summed[0],
        summed[1],
        summed[2],
        summed[3],
        summed[4],
        summed[5],
        summed[6],
        summed[7],
        summed[8],
        summed[9],
        summed[10],
        summed[11],
        summed[12],
        summed[13],
    )


def solution(mesh):
    return jax.shard_map(
        on_device,
        mesh=mesh,
        in_specs=(
            P("batch", "seq", "head"),
            P("head"),
            P(None, "head"),
            P(None, "head"),
            P(None, "head"),
            P(),
            P(None, "head"),
            P("head"),
            P(),
            P(),
            P("head"),
            P("head"),
            P("head"),
            P("head"),
            P("head", None),
            P("batch", "seq", "head"),
        ),
        out_specs=(
            P("batch", "seq", "head"),
            P("batch", "seq", "head"),
            P("head"),
            P(None, "head"),
            P(None, "head"),
            P(None, "head"),
            P(),
            P(None, "head"),
            P("head"),
            P(),
            P(),
            P("head"),
            P("head"),
            P("head"),
            P("head"),
            P("head", None),
        ),
        check_vma=False,
    )
```

profile of v0, /device:TPU:0, one launch (start us, length us, event | category | flops | bytes accessed | tf_op | source)
XLA Modules:
  0.0 855.7 jit_solution(2560668838805555344)
XLA Ops:
  13.6 7.7 all-gather.8.cloned.1.call-done
  50.1 70.7 %while.120 = (s32[]{:T(128)}, f32[1,16,64,128]{3,2,1,0:T(8,128)}, f32[2,1,256,16,64]{2,0,4,3,1:T(2,128)}, f32[2,1,256,16]{2,0,3,1:T(2,128)}, f32[16]{0:T(128)S(1...) while((s32[]{:T(128)}, f32[1,16,64,128]{3,2,1,0:T(8,128)}, ...), condition=%wide.region_4.5_spmd.clone.clone, body=%wide.region_1.4_spmd.clone.clone.sunk | while | flops 1717903360 | bytes 23170916 | solution.py:69
  53.6 4.8 fusion.317
  59.5 21.9 %dynamic_update_slice.235 = f32[2,1,256,16,64]{2,0,4,3,1:T(2,128)} dynamic-update-slice(f32[2,1,256,16,64]{2,0,4,3,1:T(2,128)} %get-tuple-element.2732, f32[1,1,256,16,64]{2,0,4,3,1:T(1,128)S(1)} %copy.413, s32[]{:T(128)} %get-tuple-element.2730, s32[]{:T(128)} %constant.258.clone.1..sunk.3, s32[]{:T(128)} %constant.258.clone.1..sunk.3, s32[]{:T(128)} %constant.258.clone.1..sunk.3, ...) | dynamic-update-slice | bytes 2097156 | tf_op jit(solution)/shard_map/vmap()/while/body/jit(dynamic_update_index_in_dim)/dynamic_update_slice | solution.py:69
  89.4 4.8 fusion.317
  95.3 21.9 %dynamic_update_slice.235 = f32[2,1,256,16,64]{2,0,4,3,1:T(2,128)} dynamic-update-slice(f32[2,1,256,16,64]{2,0,4,3,1:T(2,128)} %get-tuple-element.2732, f32[1,1,256,16,64]{2,0,4,3,1:T(1,128)S(1)} %copy.413, s32[]{:T(128)} %get-tuple-element.2730, s32[]{:T(128)} %constant.258.clone.1..sunk.3, s32[]{:T(128)} %constant.258.clone.1..sunk.3, s32[]{:T(128)} %constant.258.clone.1..sunk.3, ...) | dynamic-update-slice | bytes 2097156 | tf_op jit(solution)/shard_map/vmap()/while/body/jit(dynamic_update_index_in_dim)/dynamic_update_slice | solution.py:69
  124.2 9.4 %all_gather.29 = f32[4,1,16]{2,1,0:T(1,128)S(1)} all-gather(f32[1,1,16]{2,1,0:T(1,128)S(1)} %exp.133), channel_id=1, replica_groups=mesh['batch'=4,'seq'=4,'head'=2] {'seq'}, dimensions={0}, use_global_device_ids=true | all-gather | bytes 320 | tf_op jit(solution)/shard_map/all_gather | solution.py:24
  141.9 24.1 %all-gather.12.cloned.1.call-done = f32[4,16,64,128]{3,2,1,0:T(8,128)} async-done(((f32[1,16,64,128]{3,2,1,0:T(8,128)}), f32[4,16,64,128]{3,2,1,0:T(8,128)}) %all-gather.12.cloned.1.call-update) | async-done | bytes 2097168 | tf_op jit(solution)/shard_map/all_gather | solution.py:24
  166.0 4.8 while.118
  180.4 5.5 multiply_reduce_fusion.6
  188.5 5.9 multiply_reduce_fusion
  196.8 6.6 fusion.168
  220.1 46.4 %while.117 = (s32[]{:T(128)}, f32[1,16,64,128]{3,2,1,0:T(8,128)S(1)}, f32[2,1,256,256,16]{3,4,2,1,0:T(8,128)}, f32[2,1,128,256]{2,3,1,0:T(8,128)}, f32[2,1,256,1...) while((s32[]{:T(128)}, ...), condition=%wide.region_19.20_spmd.clone.clone, body=%wide.region_16.19_spmd.clone.clone.sunk | while | flops 912007232 | bytes 91645848 | solution.py:69
  225.2 6.3 multiply_dynamic-update-slice_fusion.4
  248.4 6.3 multiply_dynamic-update-slice_fusion.4
  271.0 4.5 copy.251
  275.5 7.3 while.119
  286.5 108.7 %while.121 = (s32[]{:T(128)}, f32[16]{0:T(128)}, f32[1,16,64,128]{3,2,1,0:T(8,128)S(1)}, f32[2,1,256,16,64]{2,4,3,1,0:T(8,128)}, f32[2,1,256,128]{3,2,1,0:T(8,12...) while((s32[]{:T(128)}, f32[16]{0:T(128)}, ...), condition=%wide.region_32.33_spmd.clone.clone, body=%wide.region_20.32_spmd.clone.clone.sunk | while | flops 3434913792 | bytes 128363696 | solution.py:69
  286.7 6.7 constant_dynamic-slice_fusion.20
  295.7 11.3 %fusion.331 = (f32[256,16]{0,1:T(8,128)}, f32[256,16]{0,1:T(8,128)}, f32[256,256]{1,0:T(8,128)S(1)}) fusion(f32[1,1,256,256,16]{3,4,2,1,0:T(8,128)S(1)} %constant_dynamic-slice_fusion.23, f32[256,256]{1,0:T(8,128)S(1)} %dynamic-slice_bitcast_fusion.8, pred[256,256]{1,0:T(8,128)(4,1)S(1)} %get-tuple-element.2976, ...), kind=kOutput, calls=%fused_computation.161.clone.1 | convolution fusion | flops 813621248 | bytes 11109376 | tf_op jit(solution)/shard_map/transpose(jvp(vmap()))/while/body/eval_jaxpr/tsh,shp->thp/dot_general | solution.py:61
  317.5 8.9 %fusion.330 = (f32[256,16]{0,1:T(8,128)S(1)}, f32[1,256,16,64]{1,3,2,0:T(8,128)}) fusion(f32[2,1,256,16,64]{2,4,3,1,0:T(8,128)} %get-tuple-element.2974, s32[]{:T(128)S(6)} %sub.235, f32[1,1,256,256,16]{3,4,2,1,0:T(8,128)} %get-tuple-element.2704, f32[2,1,256,16,64]{2,4,3,1,0:T(8,128)} %get-tuple-element.2960, ...), kind=kOutput, calls=%fused_computation.139.clone.1 | convolution fusion | flops 806350848 | bytes 8422400 | tf_op jit(solution)/shard_map/transpose(jvp(vmap()))/while/body/eval_jaxpr/tsh,shp->thp/dot_general | solution.py:61
  340.8 6.7 constant_dynamic-slice_fusion.20
  349.9 11.3 %fusion.331 = (f32[256,16]{0,1:T(8,128)}, f32[256,16]{0,1:T(8,128)}, f32[256,256]{1,0:T(8,128)S(1)}) fusion(f32[1,1,256,256,16]{3,4,2,1,0:T(8,128)S(1)} %constant_dynamic-slice_fusion.23, f32[256,256]{1,0:T(8,128)S(1)} %dynamic-slice_bitcast_fusion.8, pred[256,256]{1,0:T(8,128)(4,1)S(1)} %get-tuple-element.2976, ...), kind=kOutput, calls=%fused_computation.161.clone.1 | convolution fusion | flops 813621248 | bytes 11109376 | tf_op jit(solution)/shard_map/transpose(jvp(vmap()))/while/body/eval_jaxpr/tsh,shp->thp/dot_general | solution.py:61
  371.6 8.9 %fusion.330 = (f32[256,16]{0,1:T(8,128)S(1)}, f32[1,256,16,64]{1,3,2,0:T(8,128)}) fusion(f32[2,1,256,16,64]{2,4,3,1,0:T(8,128)} %get-tuple-element.2974, s32[]{:T(128)S(6)} %sub.235, f32[1,1,256,256,16]{3,4,2,1,0:T(8,128)} %get-tuple-element.2704, f32[2,1,256,16,64]{2,4,3,1,0:T(8,128)} %get-tuple-element.2960, ...), kind=kOutput, calls=%fused_computation.139.clone.1 | convolution fusion | flops 806350848 | bytes 8422400 | tf_op jit(solution)/shard_map/transpose(jvp(vmap()))/while/body/eval_jaxpr/tsh,shp->thp/dot_general | solution.py:61
  395.2 4.9 fusion.214
  404.0 4.9 copy.266
  408.8 4.9 reshape.1301
  413.8 6.4 fusion.222
  431.7 4.8 fusion.218
  462.0 81.9 %all-reduce.2 = (f32[512]{0:T(512)}, f32[4,1024]{1,0:T(4,128)}, f32[1024]{0:T(1024)}, f32[4,256]{1,0:T(4,128)}, f32[256]{0:T(256)}, /*index=5*/f32[16]{0:T(128)}, f32[16]{0:T(128)}, f32[16]{0:T(128)}, f32[1024]{0:T(1024)}) all-reduce(f32[512]{0:T(512)S(1)} %get-tuple-element.1965, ...), channel_id=1, replica_groups=mesh['batch'=4,'seq'=4,'head'=2] {'batch','seq'}, use_global_device_ids=true, to_apply=%region_39.40 | all-reduce | flops 7984 | bytes 63872 | tf_op jit(solution)/shard_map/psum | solution.py:261
  546.9 290.1 %all-reduce.8.cloned.1.call-done = (f32[1024,1024]{1,0:T(8,128)}, f32[1024,1024]{1,0:T(8,128)}, f32[1024,16]{0,1:T(8,128)}, f32[1024,256]{1,0:T(8,128)}, f32[1024,1024]{1,0:T(8,128)}) async-done(((f32[1024,1024]{1,0:T(8,128)}, f32[1024,1024]{1,0:T(8,128)}, f32[1024,16]{0,1:T(8,128)}, f32[1024,256]{1,0:T(8,128)}, f32[1024,1024]{1,0:T(8,128)}), (f32[1024,1024]{1,0:T(8,128)}, f32[1024,1024]{1,0:T(8,128)}, ...) | async-done | bytes 13697040 | tf_op jit(solution)/shard_map/psum | solution.py:261
  837.0 4.9 copy.557
  (611 shorter events, 252.2 us)
Async XLA Ops:
  7.2 173.2 %copy-start = (bf16[1024,1024]{1,0:T(8,128)(2,1)S(1)}, bf16[1024,1024]{1,0:T(8,128)(2,1)}, u32[]{:S(2)}) copy-start(bf16[1024,1024]{1,0:T(8,128)(2,1)} %param.28) | copy-start | bytes 6291460
  7.2 14.1 %all-gather.8.cloned.1.call-start = ((), (), s32[]{:S(2)}) async-start(), calls=%async_computation.2 | async-start | bytes 1572864 | tf_op jit(solution)/shard_map/all_gather | solution.py:132
  7.9 158.0 %all-gather.12.cloned.1.call-start = ((), (), s32[]{:S(2)}) async-start(), calls=%async_computation.6 | async-start | bytes 2621440 | tf_op jit(solution)/shard_map/all_gather | solution.py:24
  10.7 169.8 %copy-start.55 = (f32[2,1,512]{2,1,0:T(1,128)}, f32[2,1,512]{2,1,0:T(1,128)S(1)}, u32[]{:S(2)}) copy-start(f32[2,1,512]{2,1,0:T(1,128)S(1)} %convert_element_type.86) | copy-start | bytes 12292
  12.7 23.3 %copy-start.85 = (f32[1,256]{1,0:T(1,128)}, f32[1,256]{1,0:T(1,128)S(1)}, u32[]{:S(2)}) copy-start(f32[1,256]{1,0:T(1,128)S(1)} %get-tuple-element.2197) | copy-start | bytes 3076
  12.7 23.3 %copy-start.87 = (f32[1,256]{1,0:T(1,128)}, f32[1,256]{1,0:T(1,128)S(1)}, u32[]{:S(2)}) copy-start(f32[1,256]{1,0:T(1,128)S(1)} %get-tuple-element.2198) | copy-start | bytes 3076
  12.7 23.3 %copy-start.89 = (f32[1,256]{1,0:T(1,128)}, f32[1,256]{1,0:T(1,128)S(1)}, u32[]{:S(2)}) copy-start(f32[1,256]{1,0:T(1,128)S(1)} %get-tuple-element.2199) | copy-start | bytes 3076
  12.7 23.3 %copy-start.91 = (f32[1,256]{1,0:T(1,128)}, f32[1,256]{1,0:T(1,128)S(1)}, u32[]{:S(2)}) copy-start(f32[1,256]{1,0:T(1,128)S(1)} %get-tuple-element.2200) | copy-start | bytes 3076
  13.6 23.6 %copy-start.68 = (f32[1,1024]{1,0:T(1,128)}, f32[1,1024]{1,0:T(1,128)S(1)}, u32[]{:S(2)}) copy-start(f32[1,1024]{1,0:T(1,128)S(1)} %get-tuple-element.2193) | copy-start | bytes 12292
  13.6 23.6 %copy-start.70 = (f32[1,1024]{1,0:T(1,128)}, f32[1,1024]{1,0:T(1,128)S(1)}, u32[]{:S(2)}) copy-start(f32[1,1024]{1,0:T(1,128)S(1)} %get-tuple-element.2194) | copy-start | bytes 12292
  13.6 23.6 %copy-start.72 = (f32[1,1024]{1,0:T(1,128)}, f32[1,1024]{1,0:T(1,128)S(1)}, u32[]{:S(2)}) copy-start(f32[1,1024]{1,0:T(1,128)S(1)} %get-tuple-element.2195) | copy-start | bytes 12292
  13.6 23.6 %copy-start.74 = (f32[1,1024]{1,0:T(1,128)}, f32[1,1024]{1,0:T(1,128)S(1)}, u32[]{:S(2)}) copy-start(f32[1,1024]{1,0:T(1,128)S(1)} %get-tuple-element.2196) | copy-start | bytes 12292
  23.0 157.4 %copy-start.63 = (f32[512]{0:T(512)}, f32[512]{0:T(512)S(1)}, u32[]{:S(2)}) copy-start(f32[512]{0:T(512)S(1)} %add_rsqrt_fusion.1) | copy-start | bytes 6148
  24.9 11.1 %copy-start.30 = (f32[512,256]{1,0:T(8,128)}, f32[512,256]{1,0:T(8,128)S(1)}, u32[]{:S(2)}) copy-start(f32[512,256]{1,0:T(8,128)S(1)} %fusion.220) | copy-start | bytes 1572868
  24.9 9.9 %copy-start.76 = (bf16[1024,16]{0,1:T(8,128)(2,1)S(1)}, bf16[1024,16]{0,1:T(8,128)(2,1)}, u32[]{:S(2)}) copy-start(bf16[1024,16]{0,1:T(8,128)(2,1)} %param.30) | copy-start | bytes 98308
  24.9 9.9 %copy-start.100 = (f32[16]{0:T(128)S(1)}, f32[16]{0:T(128)}, u32[]{:S(2)}) copy-start(f32[16]{0:T(128)} %param.36) | copy-start | bytes 196
  24.9 11.0 %collective-permute-start.1 = (f32[1,3,256]{2,1,0:T(4,128)S(1)}, f32[1,3,256]{2,1,0:T(4,128)S(1)}, u32[]{:S(2)}, u32[]{:S(2)}) collective-permute-start(f32[1,3,256]{2,1,0:T(4,128)S(1)} %slice.201), channel_id=1, source_target_pairs={{0,2},{2,4},{4,6},{1,3},{3,5},{5,7},{8,10},{10,12},{12,14},{9,11},... | collective-permute-start | bytes 9224 | tf_op jit(solution)/shard_map/ppermute | solution.py:19
  31.4 5.8 collective-permute-start
  120.8 67.6 %all-gather.10.cloned.1.call-start = ((), (), s32[]{:S(2)}) async-start(), calls=%async_computation.4 | async-start | bytes 1572864 | tf_op jit(solution)/shard_map/all_gather | solution.py:133
  121.6 154.0 %all-gather.14.cloned.1.call-start = ((), (), s32[]{:S(2)}) async-start(), calls=%async_computation.7 | async-start | bytes 2621440 | tf_op jit(solution)/shard_map/all_gather | solution.py:24
  180.4 8.0 copy-start.61
  188.4 8.4 copy-start.78
  213.6 227.5 %all-reduce.10.cloned.1.call-start = ((), (), s32[]{:S(2)}) async-start(), calls=%async_computation.9 | async-start | bytes 1048576 | tf_op jit(solution)/shard_map/psum | solution.py:213
  317.5 13.2 %copy-start.57 = (f32[2,1,256,16,1]{2,0,4,3,1:T(2,128)S(1)}, f32[2,1,256,16,1]{2,0,4,3,1:T(2,128)}, u32[]{:S(2)}) copy-start(f32[2,1,256,16,1]{2,0,4,3,1:T(2,128)} %get-tuple-element.2966) | copy-start | bytes 98308 | tf_op jit(solution)/shard_map/transpose(jvp(vmap()))/while
  371.6 13.2 %copy-start.57 = (f32[2,1,256,16,1]{2,0,4,3,1:T(2,128)S(1)}, f32[2,1,256,16,1]{2,0,4,3,1:T(2,128)}, u32[]{:S(2)}) copy-start(f32[2,1,256,16,1]{2,0,4,3,1:T(2,128)} %get-tuple-element.2966) | copy-start | bytes 98308 | tf_op jit(solution)/shard_map/transpose(jvp(vmap()))/while
  395.2 58.2 %reduce-scatter.3.cloned.1.call-start = ((), (), s32[]{:S(2)}) async-start(), calls=%async_computation.3 | async-start | bytes 3145728 | tf_op jit(solution)/shard_map/reduce_scatter | solution.py:187
  400.2 55.8 %reduce-scatter.5.cloned.1.call-start = ((), (), s32[]{:S(2)}) async-start(), calls=%async_computation.5 | async-start | bytes 3145728 | tf_op jit(solution)/shard_map/reduce_scatter | solution.py:249
  413.8 8.0 copy-start.77
  420.3 5.6 collective-permute-start.2
  430.5 406.5 %all-reduce.8.cloned.1.call-start = ((), (), s32[]{:S(2)}) async-start(), calls=%async_computation.8 | async-start | bytes 27394048 | tf_op jit(solution)/shard_map/psum | solution.py:261
  443.6 5.5 collective-permute-start.3
  455.9 88.0 %copy-start.35 = (f32[512,512]{1,0:T(8,128)S(1)}, f32[512,512]{1,0:T(8,128)}, u32[]{:S(2)}) copy-start(f32[512,512]{1,0:T(8,128)} %reduce-scatter.5.cloned.1.call-done) | copy-start | bytes 3145732
  (124 other events, 505.1 us)
Sparse Core Ops, SparseCore 0:
  9.5 11.7 all-gather.7
  121.0 44.9 all-gather.11
  167.5 7.8 all-gather.9
  213.7 44.5 all-gather.13
  395.3 17.5 all-reduce.9
  415.0 10.8 reduce-scatter.2
  430.6 8.5 reduce-scatter.4
  451.1 385.9 all-reduce.7
where the time goes:
time: 872 us; the launch traced here: 856 us
  waiting for transfers between devices  328 us (38%)
  local copies, waits for them, and re-layouts  169 us (19%)
  matrix products  141 us (16%)
  blocking collectives  101 us (12%)
  other arithmetic  90.1 us (10%)
  between operations  15.5 us (2%)
  starting transfers between devices  10.8 us (1%)
    psum x1, waiting for transfers between devices, on_device(): lax.psum((grad_norm_gain, grad_gate_weight, grad_inner_weight, grad_step_...  290 us
    psum x1, blocking collectives, on_device(): lax.psum((grad_norm_gain, grad_gate_weight, grad_inner_weight, grad_step_...  81.9 us
    dynamic_update_slice x24, local copies, waits for them, and re-layouts, ssd_blocks(): lax.scan(advance, initial, (inner_blocks, write_blocks, read_blocks, step...  63.8 us
    dot_general x6, matrix products, advance(): jnp.einsum('tsh,shp->thp', decays * scores[:, :, None], weighted, precisi...  50 us
    unnamed x150, local copies, waits for them, and re-layouts  26.9 us
    all_gather x2, waiting for transfers between devices, entering(): everything = jax.tree.map(lambda part: lax.all_gather(part, axis), array)  24.1 us
    dynamic_slice x18, local copies, waits for them, and re-layouts, ssd_blocks(): lax.scan(advance, initial, (inner_blocks, write_blocks, read_blocks, step...  17.4 us
  transfers between devices with their start and end apart: 12, of which 5 were waited for; matrix products, arithmetic and copies ran while one was open for 18% of the time, Pallas kernels for 0%

commit v1 on v0

--- a/solution.py
+++ b/solution.py
@@ -259,23 +259,26 @@
     grad_hidden = grad_rows.reshape(seq_count, tok_count, local_width)
     grad_norm_gain = jnp.sum(input_share * normal_local, axis=0)
     summed = lax.psum(
-        (
-            grad_norm_gain,
-            grad_gate_weight,
-            grad_inner_weight,
-            grad_step_weight,
-            grad_maps_weight,
-            grad_inner_kernel,
-            grad_inner_bias,
-            grad_maps_kernel,
-            grad_maps_bias,
-            grad_step_bias,
-            grad_decay_log,
-            grad_skip_gain,
-            grad_gate_gain,
-            grad_output_weight,
+        lax.psum(
+            (
+                grad_norm_gain,
+                grad_gate_weight,
+                grad_inner_weight,
+                grad_step_weight,
+                grad_maps_weight,
+                grad_inner_kernel,
+                grad_inner_bias,
+                grad_maps_kernel,
+                grad_maps_bias,
+                grad_step_bias,
+                grad_decay_log,
+                grad_skip_gain,
+                grad_gate_gain,
+                grad_output_weight,
+            ),
+            "seq",
         ),
-        ("batch", "seq"),
+        "batch",
     )
     return (
         output,

time: 872 us -> 1240 us (1.42)
  waiting for transfers between devices: 328 us -> 734 us
  blocking collectives: 101 us -> 57.6 us
    psum x0 -> x1, waiting for transfers between devices: none -> 218 us  [on_device(): lax.psum(lax.psum((grad_norm_gain, grad_gate_weight, grad_inner_weight, g...]
    psum x1, waiting for transfers between devices: 290 us -> 451 us  [on_device(): lax.psum((grad_norm_gain, grad_gate_weight, grad_inner_weight, grad_step_...]
    psum x1, blocking collectives: 81.9 us -> 19.7 us  [on_device(): lax.psum((grad_norm_gain, grad_gate_weight, grad_inner_weight, grad_step_...]
    psum x0 -> x1, blocking collectives: none -> 19.3 us  [on_device(): lax.psum(lax.psum((grad_norm_gain, grad_gate_weight, grad_inner_weight, g...]
    unnamed x150 -> x152, local copies, waits for them, and re-layouts: 26.9 us -> 26.6 us
  transfers between devices with their start and end apart: 12 -> 13, of which waited for: 5 -> 9; matrix products, arithmetic and copies ran while one was open for 18% -> 11% of each run, Pallas kernels for 0% -> 0%
where the time goes in v1:
time: 1240 us; the launch traced here: 1220 us
  waiting for transfers between devices  734 us (59%)
  local copies, waits for them, and re-layouts  171 us (14%)
  matrix products  140 us (11%)
  other arithmetic  91.6 us (7%)
  blocking collectives  57.6 us (5%)
  between operations  15.2 us (1%)
    psum x1, waiting for transfers between devices, on_device(): lax.psum((grad_norm_gain, grad_gate_weight, grad_inner_weight, grad_step_...  451 us
    psum x1, waiting for transfers between devices, on_device(): lax.psum(lax.psum((grad_norm_gain, grad_gate_weight, grad_inner_weight, g...  218 us
    dynamic_update_slice x24, local copies, waits for them, and re-layouts, ssd_blocks(): lax.scan(advance, initial, (inner_blocks, write_blocks, read_blocks, step...  63.8 us
    dot_general x6, matrix products, advance(): jnp.einsum('tsh,shp->thp', decays * scores[:, :, None], weighted, precisi...  50 us
    unnamed x152, local copies, waits for them, and re-layouts  26.6 us
  transfers between devices with their start and end apart: 13, of which 9 were waited for; matrix products, arithmetic and copies ran while one was open for 11% of the time, Pallas kernels for 0%

profile of v1, /device:TPU:0, one launch (start us, length us, event | category | flops | bytes accessed | tf_op | source)
XLA Modules:
  0.0 1222.3 jit_solution(14390496715083658674)
XLA Ops:
  13.6 7.7 all-gather.8.cloned.1.call-done
  50.0 70.7 %while.120 = (s32[]{:T(128)}, f32[1,16,64,128]{3,2,1,0:T(8,128)}, f32[2,1,256,16,64]{2,0,4,3,1:T(2,128)}, f32[2,1,256,16]{2,0,3,1:T(2,128)}, f32[16]{0:T(128)S(1...) while((s32[]{:T(128)}, f32[1,16,64,128]{3,2,1,0:T(8,128)}, ...), condition=%wide.region_4.5_spmd.clone.clone, body=%wide.region_1.4_spmd.clone.clone.sunk | while | flops 1717903360 | bytes 23170916 | solution.py:69
  59.4 21.9 %dynamic_update_slice.235 = f32[2,1,256,16,64]{2,0,4,3,1:T(2,128)} dynamic-update-slice(f32[2,1,256,16,64]{2,0,4,3,1:T(2,128)} %get-tuple-element.2746, f32[1,1,256,16,64]{2,0,4,3,1:T(1,128)S(1)} %copy.413, s32[]{:T(128)} %get-tuple-element.2744, s32[]{:T(128)} %constant.258.clone.1..sunk.3, s32[]{:T(128)} %constant.258.clone.1..sunk.3, s32[]{:T(128)} %constant.258.clone.1..sunk.3, ...) | dynamic-update-slice | bytes 2097156 | tf_op jit(solution)/shard_map/vmap()/while/body/jit(dynamic_update_index_in_dim)/dynamic_update_slice | solution.py:69
  95.2 21.9 %dynamic_update_slice.235 = f32[2,1,256,16,64]{2,0,4,3,1:T(2,128)} dynamic-update-slice(f32[2,1,256,16,64]{2,0,4,3,1:T(2,128)} %get-tuple-element.2746, f32[1,1,256,16,64]{2,0,4,3,1:T(1,128)S(1)} %copy.413, s32[]{:T(128)} %get-tuple-element.2744, s32[]{:T(128)} %constant.258.clone.1..sunk.3, s32[]{:T(128)} %constant.258.clone.1..sunk.3, s32[]{:T(128)} %constant.258.clone.1..sunk.3, ...) | dynamic-update-slice | bytes 2097156 | tf_op jit(solution)/shard_map/vmap()/while/body/jit(dynamic_update_index_in_dim)/dynamic_update_slice | solution.py:69
  124.8 9.3 all_gather.29
  142.6 23.3 %all-gather.12.cloned.1.call-done = f32[4,16,64,128]{3,2,1,0:T(8,128)} async-done(((f32[1,16,64,128]{3,2,1,0:T(8,128)}), f32[4,16,64,128]{3,2,1,0:T(8,128)}) %all-gather.12.cloned.1.call-update) | async-done | bytes 2097168 | tf_op jit(solution)/shard_map/all_gather | solution.py:24
  180.4 5.5 multiply_reduce_fusion.6
  188.4 5.9 multiply_reduce_fusion
  196.7 6.6 fusion.168
  220.0 46.4 %while.117 = (s32[]{:T(128)}, f32[1,16,64,128]{3,2,1,0:T(8,128)S(1)}, f32[2,1,256,256,16]{3,4,2,1,0:T(8,128)}, f32[2,1,128,256]{2,3,1,0:T(8,128)}, f32[2,1,256,1...) while((s32[]{:T(128)}, ...), condition=%wide.region_19.20_spmd.clone.clone, body=%wide.region_16.19_spmd.clone.clone.sunk | while | flops 912007232 | bytes 91645848 | solution.py:69
  225.1 6.2 multiply_dynamic-update-slice_fusion.4
  248.3 6.3 multiply_dynamic-update-slice_fusion.4
  275.5 5.1 fusion.218
  284.0 7.4 while.119
  295.2 106.7 %while.121 = (s32[]{:T(128)}, f32[16]{0:T(128)}, f32[1,16,64,128]{3,2,1,0:T(8,128)S(1)}, f32[2,1,256,16,64]{2,4,3,1,0:T(8,128)}, f32[2,1,256,128]{3,2,1,0:T(8,12...) while((s32[]{:T(128)}, f32[16]{0:T(128)}, ...), condition=%wide.region_32.33_spmd.clone.clone, body=%wide.region_20.32_spmd.clone.clone.sunk | while | flops 3434913792 | bytes 128233152 | solution.py:69
  295.3 6.7 constant_dynamic-slice_fusion.20
  304.4 11.3 fusion.331
  326.2 8.9 fusion.330
  348.5 6.7 constant_dynamic-slice_fusion.20
  357.6 11.3 fusion.331
  379.4 8.9 fusion.330
  411.6 6.8 fusion.222
  425.4 5.7 fusion.162
  431.2 9.9 all-reduce.15.cloned.1.call-done
  451.8 4.9 fusion.214
  463.6 451.4 %all-reduce.11.cloned.1.call-done = (f32[1024,1024]{1,0:T(8,128)}, f32[1024,1024]{1,0:T(8,128)}, f32[1024,16]{0,1:T(8,128)}, f32[1024,256]{1,0:T(8,128)}, f32[1024,1024]{1,0:T(8,128)}) async-done(((f32[1024,1024]{1,0:T(8,128)}, f32[1024,1024]{1,0:T(8,128)}, f32[1024,16]{0,1:T(8,128)}, f32[1024,256]{1,0:T(8,128)}, f32[1024,1024]{1,0:T(8,128)}), (f32[1024,1024]{1,0:T(8,128)}, f32[1024,1024]{1,0:T(8,128)}, ...) | async-done | bytes 13697040 | tf_op jit(solution)/shard_map/psum | solution.py:262
  917.5 8.3 reduce-scatter.3.cloned.1.call-done
  928.3 10.7 reduce-scatter.5.cloned.1.call-done
  942.0 19.7 %all-reduce.2 = (f32[512]{0:T(512)S(1)}, f32[4,1024]{1,0:T(4,128)S(1)}, f32[1024]{0:T(1024)S(1)}, f32[4,256]{1,0:T(4,128)S(1)}, f32[256]{0:T(256)S(1)}, /*index=...) all-reduce(f32[512]{0:T(512)S(1)} %get-tuple-element.1965, ...), channel_id=1, replica_groups=mesh['batch'=4,'seq'=4,'head'=2] {'seq'}, use_global_device_ids=true, to_apply=%region_39.40 | all-reduce | flops 7984 | bytes 63872 | tf_op jit(solution)/shard_map/psum | solution.py:262
  961.7 19.3 %all-reduce.4 = (f32[512]{0:T(512)}, f32[4,1024]{1,0:T(4,128)}, f32[1024]{0:T(1024)}, f32[4,256]{1,0:T(4,128)}, f32[256]{0:T(256)}, /*index=5*/f32[16]{0:T(128)}, f32[16]{0:T(128)}, f32[16]{0:T(128)}, f32[1024]{0:T(1024)}) all-reduce(f32[512]{0:T(512)S(1)} %get-tuple-element.2124, ...), channel_id=1, replica_groups=mesh['batch'=4,'seq'=4,'head'=2] {'batch'}, use_global_device_ids=true, to_apply=%region_40.41 | all-reduce | flops 7984 | bytes 63872 | tf_op jit(solution)/shard_map/psum | solution.py:261
  986.5 217.5 %all-reduce.13.cloned.1.call-done = (f32[1024,1024]{1,0:T(8,128)}, f32[1024,1024]{1,0:T(8,128)}, f32[1024,16]{0,1:T(8,128)}, f32[1024,256]{1,0:T(8,128)}, f32[1024,1024]{1,0:T(8,128)}) async-done(((f32[1024,1024]{1,0:T(8,128)}, f32[1024,1024]{1,0:T(8,128)}, f32[1024,16]{0,1:T(8,128)}, f32[1024,256]{1,0:T(8,128)}, f32[1024,1024]{1,0:T(8,128)}), (f32[1024,1024]{1,0:T(8,128)}, f32[1024,1024]{1,0:T(8,128)}, ...) | async-done | bytes 13697040 | tf_op jit(solution)/shard_map/psum | solution.py:261
  1204.0 4.9 copy.562
  (621 shorter events, 277.5 us)
Async XLA Ops:
  7.2 173.2 %copy-start = (bf16[1024,1024]{1,0:T(8,128)(2,1)S(1)}, bf16[1024,1024]{1,0:T(8,128)(2,1)}, u32[]{:S(2)}) copy-start(bf16[1024,1024]{1,0:T(8,128)(2,1)} %param.28) | copy-start | bytes 6291460
  7.2 14.1 %all-gather.8.cloned.1.call-start = ((), (), s32[]{:S(2)}) async-start(), calls=%async_computation.2 | async-start | bytes 1572864 | tf_op jit(solution)/shard_map/all_gather | solution.py:132
  7.9 158.0 %all-gather.12.cloned.1.call-start = ((), (), s32[]{:S(2)}) async-start(), calls=%async_computation.6 | async-start | bytes 2621440 | tf_op jit(solution)/shard_map/all_gather | solution.py:24
  10.7 169.7 %copy-start.54 = (f32[2,1,512]{2,1,0:T(1,128)}, f32[2,1,512]{2,1,0:T(1,128)S(1)}, u32[]{:S(2)}) copy-start(f32[2,1,512]{2,1,0:T(1,128)S(1)} %convert_element_type.86) | copy-start | bytes 12292
  12.7 23.3 %copy-start.88 = (f32[1,256]{1,0:T(1,128)}, f32[1,256]{1,0:T(1,128)S(1)}, u32[]{:S(2)}) copy-start(f32[1,256]{1,0:T(1,128)S(1)} %get-tuple-element.2211) | copy-start | bytes 3076
  12.7 23.3 %copy-start.90 = (f32[1,256]{1,0:T(1,128)}, f32[1,256]{1,0:T(1,128)S(1)}, u32[]{:S(2)}) copy-start(f32[1,256]{1,0:T(1,128)S(1)} %get-tuple-element.2212) | copy-start | bytes 3076
  12.7 23.3 %copy-start.92 = (f32[1,256]{1,0:T(1,128)}, f32[1,256]{1,0:T(1,128)S(1)}, u32[]{:S(2)}) copy-start(f32[1,256]{1,0:T(1,128)S(1)} %get-tuple-element.2213) | copy-start | bytes 3076
  12.7 23.3 %copy-start.94 = (f32[1,256]{1,0:T(1,128)}, f32[1,256]{1,0:T(1,128)S(1)}, u32[]{:S(2)}) copy-start(f32[1,256]{1,0:T(1,128)S(1)} %get-tuple-element.2214) | copy-start | bytes 3076
  13.6 23.7 %copy-start.67 = (f32[1,1024]{1,0:T(1,128)}, f32[1,1024]{1,0:T(1,128)S(1)}, u32[]{:S(2)}) copy-start(f32[1,1024]{1,0:T(1,128)S(1)} %get-tuple-element.2207) | copy-start | bytes 12292
  13.6 23.7 %copy-start.69 = (f32[1,1024]{1,0:T(1,128)}, f32[1,1024]{1,0:T(1,128)S(1)}, u32[]{:S(2)}) copy-start(f32[1,1024]{1,0:T(1,128)S(1)} %get-tuple-element.2208) | copy-start | bytes 12292
  13.6 23.7 %copy-start.71 = (f32[1,1024]{1,0:T(1,128)}, f32[1,1024]{1,0:T(1,128)S(1)}, u32[]{:S(2)}) copy-start(f32[1,1024]{1,0:T(1,128)S(1)} %get-tuple-element.2209) | copy-start | bytes 12292
  13.6 23.7 %copy-start.73 = (f32[1,1024]{1,0:T(1,128)}, f32[1,1024]{1,0:T(1,128)S(1)}, u32[]{:S(2)}) copy-start(f32[1,1024]{1,0:T(1,128)S(1)} %get-tuple-element.2210) | copy-start | bytes 12292
  23.0 157.4 %copy-start.61 = (f32[512]{0:T(512)}, f32[512]{0:T(512)S(1)}, u32[]{:S(2)}) copy-start(f32[512]{0:T(512)S(1)} %add_rsqrt_fusion.1) | copy-start | bytes 6148
  24.9 11.2 copy-start.31
  24.9 9.9 copy-start.75
  24.9 11.1 collective-permute-start.1
  31.4 5.8 collective-permute-start
  50.0 72.3 %copy-start.99 = (f32[16]{0:T(128)S(1)}, f32[16]{0:T(128)}, u32[]{:S(2)}) copy-start(f32[16]{0:T(128)} %param.38) | copy-start | bytes 196
  120.8 67.6 %all-gather.10.cloned.1.call-start = ((), (), s32[]{:S(2)}) async-start(), calls=%async_computation.4 | async-start | bytes 1572864 | tf_op jit(solution)/shard_map/all_gather | solution.py:133
  121.5 162.5 %all-gather.14.cloned.1.call-start = ((), (), s32[]{:S(2)}) async-start(), calls=%async_computation.7 | async-start | bytes 2621440 | tf_op jit(solution)/shard_map/all_gather | solution.py:24
  213.4 227.6 %all-reduce.15.cloned.1.call-start = ((), (), s32[]{:S(2)}) async-start(), calls=%async_computation.10 | async-start | bytes 1048576 | tf_op jit(solution)/shard_map/psum | solution.py:213
  326.2 11.3 copy-start.85
  379.4 11.3 copy-start.85
  419.8 5.6 collective-permute-start.2
  421.3 493.7 %all-reduce.11.cloned.1.call-start = ((), (), s32[]{:S(2)}) async-start(), calls=%async_computation.8 | async-start | bytes 27394048 | tf_op jit(solution)/shard_map/psum | solution.py:262
  421.3 19.8 %copy-start.81 = (f32[1,3,256]{2,1,0:T(4,128)S(1)}, f32[1,3,256]{2,1,0:T(4,128)}, u32[]{:S(2)}) copy-start(f32[1,3,256]{2,1,0:T(4,128)} %copy-done.80) | copy-start | bytes 9220
  443.8 5.5 collective-permute-start.3
  451.1 474.6 %reduce-scatter.3.cloned.1.call-start = ((), (), s32[]{:S(2)}) async-start(), calls=%async_computation.3 | async-start | bytes 3145728 | tf_op jit(solution)/shard_map/reduce_scatter | solution.py:187
  456.7 482.3 %reduce-scatter.5.cloned.1.call-start = ((), (), s32[]{:S(2)}) async-start(), calls=%async_computation.5 | async-start | bytes 3145728 | tf_op jit(solution)/shard_map/reduce_scatter | solution.py:249
  463.5 740.5 %all-reduce.13.cloned.1.call-start = ((), (), s32[]{:S(2)}) async-start(), calls=%async_computation.9 | async-start | bytes 27394048 | tf_op jit(solution)/shard_map/psum | solution.py:261
  928.3 13.7 %copy-start.98 = (f32[1024]{0:T(1024)S(1)}, f32[1024]{0:T(1024)}, u32[]{:S(2)}) copy-start(f32[1024]{0:T(1024)} %get-tuple-element.1963) | copy-start | bytes 12292
  939.0 44.5 %copy-start.36 = (f32[512,512]{1,0:T(8,128)S(1)}, f32[512,512]{1,0:T(8,128)}, u32[]{:S(2)}) copy-start(f32[512,512]{1,0:T(8,128)} %reduce-scatter.5.cloned.1.call-done) | copy-start | bytes 3145732
  (128 other events, 565.0 us)
Sparse Core Ops, SparseCore 0:
  9.5 11.7 all-gather.7
  120.9 44.9 all-gather.11
  167.5 7.8 all-gather.9
  213.6 44.5 all-gather.13
  421.4 19.6 all-reduce.14
  451.3 463.6 all-reduce.10
  917.3 8.4 reduce-scatter.2
  928.0 10.8 reduce-scatter.4
  943.3 260.6 all-reduce.12
